TPU v7x, 32 devices: a whole 2x2x4 slice. The times are simulated.
32 devices in a mesh: fsdp: 4 (over x, core), ctx: 4 (over z), tp: 2 (over y).
Axes of the slice: x: 2, y: 2, z: 4, core: 2. Of those that a mesh axis runs over, the one named last changes fastest.
Arguments:
- layer_input: bfloat16 [4096, 2048], P(('fsdp', 'ctx', 'tp')), may hold values from -6 to 6
- cotangent: bfloat16 [4096, 2048], P(('fsdp', 'ctx', 'tp')), may hold values from -6 to 6
- lengths: int32 [4, 2], P('fsdp'), may hold values from 0 to 1024, as said below
- attn_norm: bfloat16 [2048], replicated, may hold values from 0.5 to 1.5
- query_norm_gain: bfloat16 [128], replicated, may hold values from 0.25 to 1.75
- k_norm: bfloat16 [128], replicated, may hold values from 0.25 to 1.75
- w_query: bfloat16 [2048, 2048], P('fsdp', 'tp'), may hold values from -0.125 to 0.125
- key_weight: bfloat16 [2048, 1024], P('fsdp', 'tp'), may hold values from -0.125 to 0.125
- value_weight: bfloat16 [2048, 1024], P('fsdp', 'tp'), may hold values from -0.125 to 0.125
- w_out_gate: bfloat16 [2048, 2048], P('fsdp', 'tp'), may hold values from -0.125 to 0.125
- w_output: bfloat16 [2048, 2048], P(('tp', 'fsdp')), may hold values from -2 to 2
- ffn_norm: bfloat16 [2048], replicated, may hold values from 0.5 to 1.5
- w_gate: bfloat16 [2048, 6144], P('fsdp', 'tp'), may hold values from -0.125 to 0.125
- w_up: bfloat16 [2048, 6144], P('fsdp', 'tp'), may hold values from -0.125 to 0.125
- w_down: bfloat16 [6144, 2048], P(('tp', 'fsdp')), may hold values from -0.078125 to 0.078125
Outputs:
- layer_output: bfloat16 [4096, 2048], P(('fsdp', 'ctx', 'tp'))
- input_grad: bfloat16 [4096, 2048], P(('fsdp', 'ctx', 'tp'))
- grad_attn_norm: float32 [2048], replicated
- grad_q_norm: float32 [128], replicated
- grad_k_norm: float32 [128], replicated
- grad_w_query: float32 [2048, 2048], P('fsdp', 'tp')
- grad_w_key: float32 [2048, 1024], P('fsdp', 'tp')
- grad_w_value: float32 [2048, 1024], P('fsdp', 'tp')
- grad_w_out_gate: float32 [2048, 2048], P('fsdp', 'tp')
- grad_w_output: float32 [2048, 2048], P(('tp', 'fsdp'))
- grad_ffn_norm: float32 [2048], replicated
- grad_w_gate: float32 [2048, 6144], P('fsdp', 'tp')
- grad_w_up: float32 [2048, 6144], P('fsdp', 'tp')
- grad_w_down: float32 [6144, 2048], P(('tp', 'fsdp'))
Inputs may be any that keep to these rules, and one draw needn't show every extreme that they name: `lengths`: per packed row the first count is at least 512 and the two counts add up to at most 1024; some row holds a single sequence of 1024 tokens.
All inputs are finite; a program needn't handle non-finite values.
Results may differ from a plain program's by a relative error of at most 0.024.
Values may be sent and summed in bfloat16 or wider, within the bound.
No kernel may reach another device: no remote copies, remote signals or barrier semaphores. Data moves between devices by JAX's collectives and lax.ppermute only.
A program may use at most 448 MiB of HBM per device.

v0:
```python
import jax
import jax.numpy as jnp
from jax import lax
from jax.sharding import PartitionSpec as P

HEAD_SIZE = 128
EPSILON = 1e-06
ROPE_BASE = 1000000.0
NEG_FILL = -1e30


def as_sent(value):

    def short(part):
        return part.astype(jnp.bfloat16) if part.dtype == jnp.float32 else part

    return jax.tree.map(short, value)


def apply_rms_norm(values, gain_vec):
    return (
        values * lax.rsqrt(jnp.mean(values * values, axis=-1, keepdims=True) + EPSILON) * gain_vec
    )


def norm_back(values, gain_vec, grad_in):
    row_scale = lax.rsqrt(jnp.mean(values * values, axis=-1, keepdims=True) + EPSILON)
    unit_rows = values * row_scale
    scaled = grad_in * gain_vec
    back_rows = row_scale * (
        scaled - unit_rows * jnp.mean(scaled * unit_rows, axis=-1, keepdims=True)
    )
    gain_grad = jnp.sum((grad_in * unit_rows).reshape(-1, values.shape[-1]), axis=0)
    return (back_rows, gain_grad)


def apply_rotary(values, token_position, direction):
    half_size = values.shape[-1] // 2
    frequency = jnp.power(ROPE_BASE, -jnp.arange(half_size, dtype=jnp.float32) / half_size)
    angle = token_position.astype(jnp.float32)[:, None] * frequency[None, :]
    cosine = jnp.cos(angle)[:, None, :]
    sine = direction * jnp.sin(angle)[:, None, :]
    first_half = values[..., :half_size]
    second_half = values[..., half_size:]
    return jnp.concatenate(
        [first_half * cosine - second_half * sine, second_half * cosine + first_half * sine],
        axis=-1,
    )


def segment_of(slot_ids, lengths):
    first_len = lengths[0, 0]
    second_len = lengths[0, 1]
    return jnp.where(slot_ids < first_len, 0, jnp.where(slot_ids < first_len + second_len, 1, 2))


def position_of(slot_ids, segment, lengths):
    seg_begin = jnp.where(
        segment == 0, 0, jnp.where(segment == 1, lengths[0, 0], lengths[0, 0] + lengths[0, 1])
    )
    return slot_ids - seg_begin


def to_block(local_part):
    return lax.all_gather(local_part, "tp", axis=0, tiled=True)


def to_share(partial_rows):
    return lax.psum_scatter(
        partial_rows.astype(jnp.bfloat16), "tp", scatter_dimension=0, tiled=True
    ).astype(jnp.float32)


def fold_product(left_rows, weight_set):
    pieces = jax.tree.map(
        lambda a: lax.all_gather(a, "fsdp", axis=0, tiled=True), as_sent(weight_set)
    )
    return tuple(
        (
            jnp.dot(left_rows, weight_part, preferred_element_type=jnp.float32)
            for weight_part in pieces
        )
    )


def back_product(grad_rows, weight_set):
    pieces = jax.tree.map(
        lambda a: lax.all_gather(a, "fsdp", axis=0, tiled=True), as_sent(weight_set)
    )
    result = lax.dot_general(
        grad_rows[0], pieces[0], (((1,), (1,)), ((), ())), preferred_element_type=jnp.float32
    )
    for grad_part, weight_part in zip(grad_rows[1:], pieces[1:]):
        result = result + lax.dot_general(
            grad_part, weight_part, (((1,), (1,)), ((), ())), preferred_element_type=jnp.float32
        )
    return result


def weight_grads(left_rows, grad_rows):
    widths = [grad_part.shape[1] for grad_part in grad_rows]
    shared = lax.psum_scatter(
        jnp.concatenate(
            [
                lax.dot_general(
                    left_rows,
                    grad_part,
                    (((0,), (0,)), ((), ())),
                    preferred_element_type=jnp.float32,
                )
                for grad_part in grad_rows
            ],
            axis=1,
        ).astype(jnp.bfloat16),
        "fsdp",
        scatter_dimension=0,
        tiled=True,
    )
    summed = lax.psum(shared, "ctx").astype(jnp.float32)
    pieces = []
    offset = 0
    for column_width in widths:
        pieces.append(summed[:, offset : offset + column_width])
        offset = offset + column_width
    return tuple(pieces)


def body(
    layer_input,
    cotangent,
    lengths,
    attn_norm,
    query_norm_gain,
    k_norm,
    w_query,
    key_weight,
    value_weight,
    w_out_gate,
    w_output,
    ffn_norm,
    w_gate,
    w_up,
    w_down,
):
    local_rows = layer_input.shape[0]
    block_rows = local_rows * lax.axis_size("tp")
    query_heads = w_query.shape[1] // HEAD_SIZE
    kv_heads = key_weight.shape[1] // HEAD_SIZE
    groups = query_heads // kv_heads
    score_scale = HEAD_SIZE ** (-0.5)
    block_first = lax.axis_index("ctx") * block_rows
    own_slots = (
        block_first + lax.axis_index("tp") * local_rows + jnp.arange(local_rows, dtype=jnp.int32)
    )
    own_valid = (segment_of(own_slots, lengths) < 2).astype(jnp.float32)[:, None]
    query_slots = block_first + jnp.arange(block_rows, dtype=jnp.int32)
    query_segment = segment_of(query_slots, lengths)
    query_position = position_of(query_slots, query_segment, lengths)
    inputs = layer_input.astype(jnp.float32)
    gain_one = attn_norm.astype(jnp.float32)
    gain_two = ffn_norm.astype(jnp.float32)
    query_gain = query_norm_gain.astype(jnp.float32)
    key_gain = k_norm.astype(jnp.float32)
    first_normed = to_block(apply_rms_norm(inputs, gain_one).astype(jnp.bfloat16))
    query_rows, key_projected, value_proj, gate_logits = fold_product(
        first_normed, (w_query, key_weight, value_weight, w_out_gate)
    )
    query_heads_raw = query_rows.reshape(block_rows, query_heads, HEAD_SIZE)
    key_heads_raw = key_projected.reshape(block_rows, kv_heads, HEAD_SIZE)
    query_rotated = apply_rotary(
        apply_rms_norm(query_heads_raw, query_gain), query_position, 1.0
    ).astype(jnp.bfloat16)
    key_rot = apply_rotary(apply_rms_norm(key_heads_raw, key_gain), query_position, 1.0).astype(
        jnp.bfloat16
    )
    query_grouped = query_rotated.reshape(block_rows, kv_heads, groups, HEAD_SIZE)
    key_flat = key_rot.reshape(block_rows, kv_heads * HEAD_SIZE)
    value_reduced = value_proj.astype(jnp.bfloat16)

    def key_mask(piece_rows):
        key_slots = jnp.arange(piece_rows, dtype=jnp.int32)
        key_segment = segment_of(key_slots, lengths)
        return (query_segment[:, None] == key_segment[None, :]) & (
            key_slots[None, :] <= query_slots[:, None]
        )

    head_shape = (kv_heads, groups, block_rows)
    running_top = jnp.full(head_shape + (1,), NEG_FILL, jnp.float32)
    key_piece = lax.all_gather(key_flat, "ctx", axis=0, tiled=True)
    value_piece = lax.all_gather(value_reduced, "ctx", axis=0, tiled=True)
    piece_rows = key_piece.shape[0]
    allowed = key_mask(piece_rows)
    raw_scores = jnp.einsum(
        "qhgd,khd->hgqk",
        query_grouped,
        key_piece.reshape(piece_rows, kv_heads, HEAD_SIZE),
        preferred_element_type=jnp.float32,
    )
    scores = jnp.where(allowed, raw_scores * score_scale, NEG_FILL)
    new_top = jnp.maximum(running_top, jnp.max(scores, axis=-1, keepdims=True))
    weights = jnp.where(allowed, jnp.exp(scores - new_top), 0.0)
    running_total = jnp.sum(weights, axis=-1, keepdims=True)
    mixed_sum = jnp.einsum(
        "hgqk,khd->hgqd",
        weights.astype(jnp.bfloat16),
        value_piece.reshape(piece_rows, kv_heads, HEAD_SIZE),
        preferred_element_type=jnp.float32,
    )
    mixed_sum, running_top, running_total = (mixed_sum, new_top, running_total)
    log_total = running_top + jnp.log(running_total)
    attended = jnp.transpose(mixed_sum / running_total, (2, 0, 1, 3))
    attended_rows = attended.reshape(block_rows, query_heads * HEAD_SIZE)
    gate_sig = jax.nn.sigmoid(gate_logits)
    gated_mix = (attended_rows * gate_sig).astype(jnp.bfloat16)
    attn_share = to_share(fold_product(gated_mix, (w_output,))[0])
    hidden_in = inputs + own_valid * attn_share
    normed_two = to_block(apply_rms_norm(hidden_in, gain_two).astype(jnp.bfloat16))
    gate_pre, up_pre = fold_product(normed_two, (w_gate, w_up))
    gate_sigmoid = jax.nn.sigmoid(gate_pre)
    activated = gate_pre * gate_sigmoid
    hidden_act = (activated * up_pre).astype(jnp.bfloat16)
    ffn_share = to_share(fold_product(hidden_act, (w_down,))[0])
    layer_output = (hidden_in + own_valid * ffn_share).astype(jnp.bfloat16)
    out_grad = cotangent.astype(jnp.float32) * own_valid
    ffn_grad = to_block(out_grad.astype(jnp.bfloat16))
    hidden_grad = back_product((ffn_grad,), (w_down,))
    grad_w_down = weight_grads(hidden_act, (ffn_grad,))[0]
    gate_grad = (
        hidden_grad * up_pre * gate_sigmoid * (1.0 + gate_pre * (1.0 - gate_sigmoid))
    ).astype(jnp.bfloat16)
    up_grad = (hidden_grad * activated).astype(jnp.bfloat16)
    normed_two_grad = to_share(back_product((gate_grad, up_grad), (w_gate, w_up)))
    grad_w_gate, grad_w_up = weight_grads(normed_two, (gate_grad, up_grad))
    back_two, gain_two_grad = norm_back(hidden_in, gain_two, normed_two_grad)
    hidden_total_grad = out_grad + back_two
    attn_grad = to_block((own_valid * hidden_total_grad).astype(jnp.bfloat16))
    gated_grad = back_product((attn_grad,), (w_output,))
    grad_w_output = weight_grads(gated_mix, (attn_grad,))[0]
    mixed_grad = (gated_grad * gate_sig).astype(jnp.bfloat16)
    gate_logit_grad = (gated_grad * attended_rows * gate_sig * (1.0 - gate_sig)).astype(
        jnp.bfloat16
    )
    mixed_grad_heads = mixed_grad.reshape(block_rows, kv_heads, groups, HEAD_SIZE)
    delta_rows = jnp.transpose(
        jnp.sum(mixed_grad_heads.astype(jnp.float32) * attended, axis=-1), (1, 2, 0)
    )[..., None]
    key_piece = lax.all_gather(key_flat, "ctx", axis=0, tiled=True)
    value_piece = lax.all_gather(value_reduced, "ctx", axis=0, tiled=True)
    piece_rows = key_piece.shape[0]
    key_view = key_piece.reshape(piece_rows, kv_heads, HEAD_SIZE)
    value_view = value_piece.reshape(piece_rows, kv_heads, HEAD_SIZE)
    allowed = key_mask(piece_rows)
    raw_scores = jnp.einsum(
        "qhgd,khd->hgqk", query_grouped, key_view, preferred_element_type=jnp.float32
    )
    soft_vals = jnp.where(allowed, jnp.exp(raw_scores * score_scale - log_total), 0.0)
    prob_grad = jnp.einsum(
        "qhgd,khd->hgqk", mixed_grad_heads, value_view, preferred_element_type=jnp.float32
    )
    score_grad = (soft_vals * (prob_grad - delta_rows) * score_scale).astype(jnp.bfloat16)
    query_acc = jnp.einsum(
        "hgqk,khd->qhgd", score_grad, key_view, preferred_element_type=jnp.float32
    )
    key_part = jnp.einsum(
        "hgqk,qhgd->khd", score_grad, query_grouped, preferred_element_type=jnp.float32
    ).reshape(piece_rows, kv_heads * HEAD_SIZE)
    value_part = jnp.einsum(
        "hgqk,qhgd->khd",
        soft_vals.astype(jnp.bfloat16),
        mixed_grad_heads,
        preferred_element_type=jnp.float32,
    ).reshape(piece_rows, kv_heads * HEAD_SIZE)
    kv_acc = jnp.concatenate([key_part, value_part], axis=1)
    query_acc, kv_acc = (query_acc, kv_acc)
    kv_own = lax.psum_scatter(
        kv_acc.astype(jnp.bfloat16), "ctx", scatter_dimension=0, tiled=True
    ).astype(jnp.float32)
    key_rot_grad = kv_own[:, : kv_heads * HEAD_SIZE].reshape(block_rows, kv_heads, HEAD_SIZE)
    value_grad = kv_own[:, kv_heads * HEAD_SIZE :].astype(jnp.bfloat16)
    key_back, key_gain_grad = norm_back(
        key_heads_raw, key_gain, apply_rotary(key_rot_grad, query_position, -1.0)
    )
    query_back, query_gain_grad = norm_back(
        query_heads_raw,
        query_gain,
        apply_rotary(query_acc.reshape(block_rows, query_heads, HEAD_SIZE), query_position, -1.0),
    )
    query_grad = query_back.reshape(block_rows, query_heads * HEAD_SIZE).astype(jnp.bfloat16)
    key_grad = key_back.reshape(block_rows, kv_heads * HEAD_SIZE).astype(jnp.bfloat16)
    attn_in_grads = (query_grad, key_grad, value_grad, gate_logit_grad)
    normed_one_grad = to_share(
        back_product(attn_in_grads, (w_query, key_weight, value_weight, w_out_gate))
    )
    grad_w_query, grad_w_key, grad_w_value, grad_w_out_gate = weight_grads(
        first_normed, attn_in_grads
    )
    back_one, gain_one_grad = norm_back(inputs, gain_one, normed_one_grad)
    input_grad = (hidden_total_grad + back_one).astype(jnp.bfloat16)
    gain_totals = lax.psum(
        (gain_one_grad, query_gain_grad, key_gain_grad, gain_two_grad), ("fsdp", "ctx", "tp")
    )
    return (
        layer_output,
        input_grad,
        gain_totals[0],
        gain_totals[1],
        gain_totals[2],
        grad_w_query,
        grad_w_key,
        grad_w_value,
        grad_w_out_gate,
        grad_w_output,
        gain_totals[3],
        grad_w_gate,
        grad_w_up,
        grad_w_down,
    )


def solution(mesh):
    return jax.shard_map(
        body,
        mesh=mesh,
        in_specs=(
            P(("fsdp", "ctx", "tp"), None),
            P(("fsdp", "ctx", "tp"), None),
            P("fsdp", None),
            P(),
            P(),
            P(),
            P("fsdp", "tp"),
            P("fsdp", "tp"),
            P("fsdp", "tp"),
            P("fsdp", "tp"),
            P(("tp", "fsdp"), None),
            P(),
            P("fsdp", "tp"),
            P("fsdp", "tp"),
            P(("tp", "fsdp"), None),
        ),
        out_specs=(
            P(("fsdp", "ctx", "tp"), None),
            P(("fsdp", "ctx", "tp"), None),
            P(),
            P(),
            P(),
            P("fsdp", "tp"),
            P("fsdp", "tp"),
            P("fsdp", "tp"),
            P("fsdp", "tp"),
            P(("tp", "fsdp"), None),
            P(),
            P("fsdp", "tp"),
            P("fsdp", "tp"),
            P(("tp", "fsdp"), None),
        ),
        check_vma=False,
    )
```

profile of v0, /device:TPU:0, one launch (start us, length us, event | category | flops | bytes accessed | tf_op | source)
XLA Modules:
  0.0 1699.3 jit_solution(15141842273888128146)
XLA Ops:
  12.8 22.6 %all-gather.15.cloned.1.call-done = bf16[256,2048]{1,0:T(8,128)(2,1)} async-done(((bf16[128,2048]{1,0:T(8,128)(2,1)}), bf16[256,2048]{1,0:T(8,128)(2,1)}) %all-gather.15.cloned.1.call-update) | async-done | bytes 1048592 | tf_op jit(solution)/shard_map/all_gather | solution.py:65
  35.4 24.1 %all-gather.23.cloned.1.call-done = bf16[2048,512]{1,0:T(8,128)(2,1)} async-done(((bf16[512,512]{1,0:T(8,128)(2,1)}), bf16[2048,512]{1,0:T(8,128)(2,1)}) %all-gather.23.cloned.1.call-update) | async-done | bytes 2097168 | tf_op jit(solution)/shard_map/all_gather | solution.py:76
  67.3 16.4 all-gather.17.cloned.1.call-done
  92.2 21.5 %all-gather.25.cloned.1.call-done = bf16[1024,512]{1,0:T(8,128)(2,1)} async-done(((bf16[256,512]{1,0:T(8,128)(2,1)}), bf16[1024,512]{1,0:T(8,128)(2,1)}) %all-gather.25.cloned.1.call-update) | async-done | bytes 1048592 | tf_op jit(solution)/shard_map/all_gather | solution.py:190
  115.9 33.1 %all-gather.21.cloned.1.call-done = bf16[2048,1024]{1,0:T(8,128)(2,1)} async-done(((bf16[512,1024]{1,0:T(8,128)(2,1)}), bf16[2048,1024]{1,0:T(8,128)(2,1)}) %all-gather.21.cloned.1.call-update) | async-done | bytes 4194320 | tf_op jit(solution)/shard_map/all_gather | solution.py:76
  155.1 25.9 %all-gather.19.cloned.1.call-done = bf16[1024,512]{0,1:T(8,128)(2,1)} async-done(((bf16[256,512]{0,1:T(8,128)(2,1)}), bf16[1024,512]{0,1:T(8,128)(2,1)}) %all-gather.19.cloned.1.call-update) | async-done | bytes 1048592 | tf_op jit(solution)/shard_map/all_gather | solution.py:189
  193.8 21.5 %all-gather.27.cloned.1.call-done = bf16[2048,1024]{1,0:T(8,128)(2,1)} async-done(((bf16[512,1024]{1,0:T(8,128)(2,1)}), bf16[2048,1024]{1,0:T(8,128)(2,1)}) %all-gather.27.cloned.1.call-update) | async-done | bytes 4194320 | tf_op jit(solution)/shard_map/all_gather | solution.py:76
  220.3 31.1 %all-gather.29.cloned.1.call-done = bf16[1024,2048]{1,0:T(8,128)(2,1)} async-done(((bf16[256,2048]{1,0:T(8,128)(2,1)}), bf16[1024,2048]{1,0:T(8,128)(2,1)}) %all-gather.29.cloned.1.call-update) | async-done | bytes 4194320 | tf_op jit(solution)/shard_map/all_gather | solution.py:76
  258.0 18.6 %reduce-scatter.10.cloned.1.call-done = bf16[128,2048]{1,0:T(8,128)(2,1)} async-done(((bf16[256,2048]{1,0:T(8,128)(2,1)}), bf16[128,2048]{1,0:T(8,128)(2,1)}) %reduce-scatter.10.cloned.1.call-update) | async-done | bytes 524304 | tf_op jit(solution)/shard_map/reduce_scatter | solution.py:69
  283.6 18.2 %all-gather.31.cloned.1.call-done = bf16[256,2048]{1,0:T(8,128)(2,1)} async-done(((bf16[128,2048]{1,0:T(8,128)(2,1)}), bf16[256,2048]{1,0:T(8,128)(2,1)}) %all-gather.31.cloned.1.call-update) | async-done | bytes 1048592 | tf_op jit(solution)/shard_map/all_gather | solution.py:65
  301.8 83.7 %all-gather.33.cloned.1.call-done = bf16[2048,3072]{1,0:T(8,128)(2,1)} async-done(((bf16[512,3072]{1,0:T(8,128)(2,1)}), bf16[2048,3072]{1,0:T(8,128)(2,1)}) %all-gather.33.cloned.1.call-update) | async-done | bytes 12582928 | tf_op jit(solution)/shard_map/all_gather | solution.py:76
  385.5 10.0 fusion.83
  395.4 73.5 %all-gather.35.cloned.1.call-done = bf16[2048,3072]{1,0:T(8,128)(2,1)} async-done(((bf16[512,3072]{1,0:T(8,128)(2,1)}), bf16[2048,3072]{1,0:T(8,128)(2,1)}) %all-gather.35.cloned.1.call-update) | async-done | bytes 12582928 | tf_op jit(solution)/shard_map/all_gather | solution.py:76
  469.0 10.0 fusion.84
  479.0 13.4 all-gather.39.cloned.1.call-done
  492.4 83.6 %all-gather.37.cloned.1.call-done = bf16[3072,2048]{1,0:T(8,128)(2,1)} async-done(((bf16[768,2048]{1,0:T(8,128)(2,1)}), bf16[3072,2048]{1,0:T(8,128)(2,1)}) %all-gather.37.cloned.1.call-update) | async-done | bytes 12582928 | tf_op jit(solution)/shard_map/all_gather | solution.py:76
  576.0 13.4 multiply_convert_fusion
  596.5 9.1 fusion.20
  605.7 20.5 %reduce-scatter.14.cloned.1.call-done = bf16[128,2048]{1,0:T(8,128)(2,1)} async-done(((bf16[256,2048]{1,0:T(8,128)(2,1)}), bf16[128,2048]{1,0:T(8,128)(2,1)}) %reduce-scatter.14.cloned.1.call-update) | async-done | bytes 524304 | tf_op jit(solution)/shard_map/reduce_scatter | solution.py:69
  632.8 20.1 %all-gather.41.cloned.1.call-done = bf16[256,2048]{1,0:T(8,128)(2,1)} async-done(((bf16[128,2048]{1,0:T(8,128)(2,1)}), bf16[256,2048]{1,0:T(8,128)(2,1)}) %all-gather.41.cloned.1.call-update) | async-done | bytes 1048592 | tf_op jit(solution)/shard_map/all_gather | solution.py:65
  683.2 10.1 convolution_convert_fusion
  734.8 29.6 %pad_maximum_fusion.1 = bf16[2048,3072]{0,1:T(8,128)(2,1)} fusion(bf16[2048,1024]{0,1:T(8,128)(2,1)S(1)} %copy-done.3, bf16[2048,512]{0,1:T(8,128)(2,1)S(1)} %convolution_convert_fusion.6, bf16[2048,512]{0,1:T(8,128)(2,1)S(1)} %convolution_convert_fusion.7, bf16[2048,1024]{0,1:T(8,128)(2,1)S(1)} %copy-done.4), kind=kLoop, calls=%fused_computation.1 | loop fusion | flops 50331648 | bytes 25165824 | tf_op jit(solution)/shard_map/concatenate | solution.py:103
  773.6 8.4 convolution_convert_fusion.2
  782.0 20.1 %pad_maximum_fusion = bf16[2048,6144]{1,0:T(8,128)(2,1)} fusion(bf16[2048,3072]{1,0:T(8,128)(2,1)} %convolution_convert_fusion.1, bf16[2048,3072]{1,0:T(8,128)(2,1)} %convolution_convert_fusion.2), kind=kLoop, calls=%fused_computation | loop fusion | flops 50331648 | bytes 50331648 | tf_op jit(solution)/shard_map/concatenate | solution.py:103
  811.9 9.7 convolution_convert_fusion.9
  821.7 49.5 %reduce-scatter.26.cloned.1.call-done = bf16[768,2048]{1,0:T(8,128)(2,1)} async-done(((bf16[3072,2048]{1,0:T(8,128)(2,1)}), bf16[768,2048]{1,0:T(8,128)(2,1)}) %reduce-scatter.26.cloned.1.call-update) | async-done | bytes 3145744 | tf_op jit(solution)/shard_map/reduce_scatter | solution.py:102
  871.2 99.6 %reduce-scatter.20.cloned.1.call-done = bf16[512,3072]{0,1:T(8,128)(2,1)} async-done(((bf16[2048,3072]{0,1:T(8,128)(2,1)}), bf16[512,3072]{0,1:T(8,128)(2,1)}) %reduce-scatter.20.cloned.1.call-update) | async-done | bytes 3145744 | tf_op jit(solution)/shard_map/reduce_scatter | solution.py:102
  970.8 184.5 %reduce-scatter.24.cloned.1.call-done = bf16[512,6144]{1,0:T(8,128)(2,1)} async-done(((bf16[2048,6144]{1,0:T(8,128)(2,1)}), bf16[512,6144]{1,0:T(8,128)(2,1)}) %reduce-scatter.24.cloned.1.call-update) | async-done | bytes 6291472 | tf_op jit(solution)/shard_map/reduce_scatter | solution.py:102
  1163.6 15.0 reduce-scatter.18.cloned.1.call-done
  1180.1 40.4 %all-reduce = (f32[2048]{0:T(1024)}, f32[128]{0:T(128)}, f32[128]{0:T(128)}, f32[2048]{0:T(1024)}) all-reduce(f32[2048]{0:T(1024)S(1)} %get-tuple-element.44, f32[128]{0:T(128)S(1)} %fusion.51, f32[128]{0:T(128)S(1)} %fusion.62, f32[2048]{0:T(1024)S(1)} %copy-done.46), channel_id=1, replica_groups=mesh['fsdp'=4,'ctx'=4,'tp'=2] {'fsdp','ctx','tp'}, use_global_device_ids=true, to_apply=%region_17.18 | all-reduce | flops 4352 | bytes 34816 | tf_op jit(solution)/shard_map/psum | solution.py:299
  1223.9 440.9 %all-reduce.4.cloned.1.call-done = (bf16[512,3072]{0,1:T(8,128)(2,1)}, bf16[512,6144]{1,0:T(8,128)(2,1)}, bf16[256,2048]{1,0:T(8,128)(2,1)}, bf16[768,2048]{1,0:T(8,128)(2,1)}) async-done(((bf16[512,3072]{0,1:T(8,128)(2,1)}, bf16[512,6144]{1,0:T(8,128)(2,1)}, bf16[256,2048]{1,0:T(8,128)(2,1)}, bf16[768,2048]{1,0:T(8,128)(2,1)}), (bf16[512,3072]{0,1:T(8,128)(2,1)}, bf16[512,6144]{1,0:T(8,128)(2,1)}, ...) | async-done | bytes 13631504 | tf_op jit(solution)/shard_map/psum | solution.py:119
  1679.3 9.4 fusion.75
  (285 shorter events, 195.0 us)
Async XLA Ops:
  7.2 56.4 %copy-start.63 = (bf16[128]{0:T(256)(128)(2,1)S(1)}, bf16[128]{0:T(256)(128)(2,1)}, u32[]{:S(2)}) copy-start(bf16[128]{0:T(256)(128)(2,1)} %param.20) | copy-start | bytes 772
  7.2 56.4 %copy-start.59 = (s32[1,2]{1,0:T(1,128)S(1)}, s32[1,2]{1,0:T(1,128)}, u32[]{:S(2)}) copy-start(s32[1,2]{1,0:T(1,128)} %param.17) | copy-start | bytes 28
  7.2 28.2 %all-gather.15.cloned.1.call-start = ((), (), s32[]{:S(2)}) async-start(), calls=%async_computation.9 | async-start | bytes 1572864 | tf_op jit(solution)/shard_map/all_gather | solution.py:65
  11.2 48.3 %all-gather.23.cloned.1.call-start = ((), (), s32[]{:S(2)}) async-start(), calls=%async_computation.13 | async-start | bytes 2621440 | tf_op jit(solution)/shard_map/all_gather | solution.py:76
  12.0 71.7 %all-gather.17.cloned.1.call-start = ((), (), s32[]{:S(2)}) async-start(), calls=%async_computation.10 | async-start | bytes 2621440 | tf_op jit(solution)/shard_map/all_gather | solution.py:76
  12.7 101.0 %all-gather.25.cloned.1.call-start = ((), (), s32[]{:S(2)}) async-start(), calls=%async_computation.14 | async-start | bytes 1310720 | tf_op jit(solution)/shard_map/all_gather | solution.py:190
  62.9 86.1 %all-gather.21.cloned.1.call-start = ((), (), s32[]{:S(2)}) async-start(), calls=%async_computation.12 | async-start | bytes 5242880 | tf_op jit(solution)/shard_map/all_gather | solution.py:76
  63.5 117.5 %all-gather.19.cloned.1.call-start = ((), (), s32[]{:S(2)}) async-start(), calls=%async_computation.11 | async-start | bytes 1310720 | tf_op jit(solution)/shard_map/all_gather | solution.py:189
  67.3 87.1 %copy-start.27 = (f32[256,64]{1,0:T(8,128)}, f32[256,64]{1,0:T(8,128)S(1)}, u32[]{:S(2)}) copy-start(f32[256,64]{1,0:T(8,128)S(1)} %get-tuple-element.85) | copy-start | bytes 196612
  88.8 126.6 %all-gather.27.cloned.1.call-start = ((), (), s32[]{:S(2)}) async-start(), calls=%async_computation.15 | async-start | bytes 5242880 | tf_op jit(solution)/shard_map/all_gather | solution.py:76
  89.5 161.9 %all-gather.29.cloned.1.call-start = ((), (), s32[]{:S(2)}) async-start(), calls=%async_computation.16 | async-start | bytes 5242880 | tf_op jit(solution)/shard_map/all_gather | solution.py:76
  90.3 186.3 %reduce-scatter.10.cloned.1.call-start = ((), (), s32[]{:S(2)}) async-start(), calls=%async_computation.17 | async-start | bytes 1572864 | tf_op jit(solution)/shard_map/reduce_scatter | solution.py:69
  90.6 63.4 %copy-start.57 = (f32[128]{0:T(128)}, f32[128]{0:T(128)S(1)}, u32[]{:S(2)}) copy-start(f32[128]{0:T(128)S(1)} %convert_element_type.153) | copy-start | bytes 1540
  220.3 56.3 %copy-start.1 = (bf16[128,2048]{1,0:T(8,128)(2,1)S(1)}, bf16[128,2048]{1,0:T(8,128)(2,1)}, u32[]{:S(2)}) copy-start(bf16[128,2048]{1,0:T(8,128)(2,1)} %param.15) | copy-start | bytes 1572868
  256.0 45.8 %all-gather.31.cloned.1.call-start = ((), (), s32[]{:S(2)}) async-start(), calls=%async_computation.18 | async-start | bytes 1572864 | tf_op jit(solution)/shard_map/all_gather | solution.py:65
  280.4 105.1 %all-gather.33.cloned.1.call-start = ((), (), s32[]{:S(2)}) async-start(), calls=%async_computation.19 | async-start | bytes 15728640 | tf_op jit(solution)/shard_map/all_gather | solution.py:76
  281.1 187.9 %all-gather.35.cloned.1.call-start = ((), (), s32[]{:S(2)}) async-start(), calls=%async_computation.20 | async-start | bytes 15728640 | tf_op jit(solution)/shard_map/all_gather | solution.py:76
  281.7 210.7 %all-gather.39.cloned.1.call-start = ((), (), s32[]{:S(2)}) async-start(), calls=%async_computation.23 | async-start | bytes 1572864 | tf_op jit(solution)/shard_map/all_gather | solution.py:65
  282.4 293.6 %all-gather.37.cloned.1.call-start = ((), (), s32[]{:S(2)}) async-start(), calls=%async_computation.21 | async-start | bytes 15728640 | tf_op jit(solution)/shard_map/all_gather | solution.py:76
  283.0 343.2 %reduce-scatter.14.cloned.1.call-start = ((), (), s32[]{:S(2)}) async-start(), calls=%async_computation.24 | async-start | bytes 1572864 | tf_op jit(solution)/shard_map/reduce_scatter | solution.py:69
  605.6 47.3 %all-gather.41.cloned.1.call-start = ((), (), s32[]{:S(2)}) async-start(), calls=%async_computation.25 | async-start | bytes 1572864 | tf_op jit(solution)/shard_map/all_gather | solution.py:65
  631.5 90.7 %reduce-scatter.16.cloned.1.call-start = ((), (), s32[]{:S(2)}) async-start(), calls=%async_computation.26 | async-start | bytes 2621440 | tf_op jit(solution)/shard_map/reduce_scatter | solution.py:275
  678.4 143.3 %reduce-scatter.22.cloned.1.call-start = ((), (), s32[]{:S(2)}) async-start(), calls=%async_computation.29 | async-start | bytes 5242880 | tf_op jit(solution)/shard_map/reduce_scatter | solution.py:102
  683.1 188.0 %reduce-scatter.26.cloned.1.call-start = ((), (), s32[]{:S(2)}) async-start(), calls=%async_computation.31 | async-start | bytes 15728640 | tf_op jit(solution)/shard_map/reduce_scatter | solution.py:102
  693.3 277.5 %reduce-scatter.20.cloned.1.call-start = ((), (), s32[]{:S(2)}) async-start(), calls=%async_computation.28 | async-start | bytes 15728640 | tf_op jit(solution)/shard_map/reduce_scatter | solution.py:102
  764.4 390.9 %reduce-scatter.24.cloned.1.call-start = ((), (), s32[]{:S(2)}) async-start(), calls=%async_computation.30 | async-start | bytes 31457280 | tf_op jit(solution)/shard_map/reduce_scatter | solution.py:102
  802.1 376.5 %reduce-scatter.18.cloned.1.call-start = ((), (), s32[]{:S(2)}) async-start(), calls=%async_computation.27 | async-start | bytes 1572864 | tf_op jit(solution)/shard_map/reduce_scatter | solution.py:69
  811.8 408.6 %reduce-scatter.12.cloned.1.call-start = ((), (), s32[]{:S(2)}) async-start(), calls=%async_computation.22 | async-start | bytes 1572864 | tf_op jit(solution)/shard_map/reduce_scatter | solution.py:69
  821.6 843.2 %all-reduce.4.cloned.1.call-start = ((), (), s32[]{:S(2)}) async-start(), calls=%async_computation.32 | async-start | bytes 27262976 | tf_op jit(solution)/shard_map/psum | solution.py:119
  1157.4 63.1 %copy-start.48 = (f32[128]{0:T(128)S(1)}, f32[128]{0:T(128)}, u32[]{:S(2)}) copy-start(f32[128]{0:T(128)} %compare_convert_fusion) | copy-start | bytes 1540
  1157.4 63.1 %copy-start.51 = (f32[128]{0:T(128)S(1)}, f32[128]{0:T(128)}, u32[]{:S(2)}) copy-start(f32[128]{0:T(128)} %copy-done.50) | copy-start | bytes 1540
  1157.4 63.1 %copy-start.61 = (f32[128]{0:T(128)S(1)}, f32[128]{0:T(128)}, u32[]{:S(2)}) copy-start(f32[128]{0:T(128)} %copy-done.60) | copy-start | bytes 1540
  (57 other events, 487.8 us)
Sparse Core Ops, SparseCore 0:
  11.4 23.9 all-gather.14
  37.0 22.5 all-gather.22
  61.1 22.5 all-gather.16
  85.7 27.9 all-gather.24
  115.2 33.8 all-gather.20
  151.0 29.9 all-gather.18
  182.5 32.7 all-gather.26
  216.9 34.4 all-gather.28
  256.1 20.3 reduce-scatter.9
  280.5 21.2 all-gather.30
  303.4 82.0 all-gather.32
  386.9 82.0 all-gather.34
  471.1 21.2 all-gather.38
  493.8 82.1 all-gather.36
  605.7 20.3 reduce-scatter.13
  631.6 21.2 all-gather.40
  678.5 43.6 reduce-scatter.15
  725.1 43.7 reduce-scatter.21
  771.5 99.6 reduce-scatter.25
  873.6 97.1 reduce-scatter.19
  973.4 181.8 reduce-scatter.23
  1158.1 20.3 reduce-scatter.17
  1181.4 20.5 reduce-scatter.11
  1204.8 459.9 all-reduce.3
where the time goes:
time: 1700 us
  waiting for transfers between devices  1330 us (78%)
  matrix products  153 us (9%)
  other arithmetic  98.6 us (6%)
  local copies, waits for them, and re-layouts  58.1 us (3%)
  blocking collectives  40.4 us (2%)
    psum x1, waiting for transfers between devices, weight_grads(): summed = lax.psum(shared, 'ctx').astype(jnp.float32)  441 us
    all_gather x8, waiting for transfers between devices, fold_product(): lax.all_gather(a, 'fsdp', axis=0, tiled=True)  367 us
    reduce_scatter x4, waiting for transfers between devices, weight_grads(): lax.psum_scatter(jnp.concatenate([lax.dot_general(left_rows, grad_part, (...  334 us
    all_gather x4, waiting for transfers between devices, to_block(): return lax.all_gather(local_part, 'tp', axis=0, tiled=True)  74.3 us
    reduce_scatter x4, waiting for transfers between devices, to_share(): lax.psum_scatter(partial_rows.astype(jnp.bfloat16), 'tp', scatter_dimensi...  54.1 us
    concatenate x2, other arithmetic, weight_grads(): jnp.concatenate([lax.dot_general(left_rows, grad_part, (((0,), (0,)), (()...  49.7 us
    dot_general x8, matrix products, fold_product(): jnp.dot(left_rows, weight_part, preferred_element_type=jnp.float32)  48.3 us
    psum x1, blocking collectives, body(): lax.psum((gain_one_grad, query_gain_grad, key_gain_grad, gain_two_grad),...  40.4 us
  transfers between devices with their start and end apart: 24, of which 22 were waited for; matrix products, arithmetic and copies ran while one was open for 12% of the time, Pallas kernels for 0%

commit v1 on v0

--- a/solution.py
+++ b/solution.py
@@ -7,6 +7,10 @@
 EPSILON = 1e-06
 ROPE_BASE = 1000000.0
 NEG_FILL = -1e30
+
+
+def sectors_rest(work_x):
+    return lax.all_gather(work_x, "ctx").sum(axis=0)
 
 
 def as_sent(value):
@@ -116,7 +120,7 @@
         scatter_dimension=0,
         tiled=True,
     )
-    summed = lax.psum(shared, "ctx").astype(jnp.float32)
+    summed = sectors_rest(shared).astype(jnp.float32)
     pieces = []
     offset = 0
     for column_width in widths:

time: 1700 us -> 2190 us (1.29)
  waiting for transfers between devices: 1330 us -> 1740 us
  other arithmetic: 98.6 us -> 148 us
  local copies, waits for them, and re-layouts: 58.1 us -> 81.9 us
    all_gather x0 -> x4, waiting for transfers between devices: none -> 848 us  [sectors_rest(): return lax.all_gather(work_x, 'ctx').sum(axis=0)]
    psum x1 -> x0, waiting for transfers between devices: 441 us -> none  [weight_grads(): summed = lax.psum(shared, 'ctx').astype(jnp.float32)]
    reduce_sum x0 -> x4, other arithmetic: none -> 49.5 us  [sectors_rest(): return lax.all_gather(work_x, 'ctx').sum(axis=0)]
    all_gather x0 -> x1, local copies, waits for them, and re-layouts: none -> 22 us  [sectors_rest(): return lax.all_gather(work_x, 'ctx').sum(axis=0)]
  transfers between devices with their start and end apart: 24 -> 27, of which waited for: 22 -> 25; matrix products, arithmetic and copies ran while one was open for 12% -> 13% of each run, Pallas kernels for 0% -> 0%
where the time goes in v1:
time: 2190 us; the launch traced here: 2180 us
  waiting for transfers between devices  1740 us (79%)
  matrix products  152 us (7%)
  other arithmetic  148 us (7%)
  local copies, waits for them, and re-layouts  81.9 us (4%)
  blocking collectives  40.3 us (2%)
    all_gather x4, waiting for transfers between devices, sectors_rest(): return lax.all_gather(work_x, 'ctx').sum(axis=0)  848 us
    all_gather x8, waiting for transfers between devices, fold_product(): lax.all_gather(a, 'fsdp', axis=0, tiled=True)  367 us
    reduce_scatter x4, waiting for transfers between devices, weight_grads(): lax.psum_scatter(jnp.concatenate([lax.dot_general(left_rows, grad_part, (...  333 us
    all_gather x4, waiting for transfers between devices, to_block(): return lax.all_gather(local_part, 'tp', axis=0, tiled=True)  74.7 us
    reduce_scatter x4, waiting for transfers between devices, to_share(): lax.psum_scatter(partial_rows.astype(jnp.bfloat16), 'tp', scatter_dimensi...  54.2 us
    concatenate x2, other arithmetic, weight_grads(): jnp.concatenate([lax.dot_general(left_rows, grad_part, (((0,), (0,)), (()...  49.8 us
    reduce_sum x4, other arithmetic, sectors_rest(): return lax.all_gather(work_x, 'ctx').sum(axis=0)  49.5 us
    dot_general x8, matrix products, fold_product(): jnp.dot(left_rows, weight_part, preferred_element_type=jnp.float32)  48.3 us
  transfers between devices with their start and end apart: 27, of which 25 were waited for; matrix products, arithmetic and copies ran while one was open for 13% of the time, Pallas kernels for 0%

profile of v1, /device:TPU:0, one launch (start us, length us, event | category | flops | bytes accessed | tf_op | source)
XLA Modules:
  0.0 2179.9 jit_solution(6096626165355810287)
XLA Ops:
  13.3 22.6 %all-gather.23.cloned.1.call-done = bf16[256,2048]{1,0:T(8,128)(2,1)} async-done(((bf16[128,2048]{1,0:T(8,128)(2,1)}), bf16[256,2048]{1,0:T(8,128)(2,1)}) %all-gather.23.cloned.1.call-update) | async-done | bytes 1048592 | tf_op jit(solution)/shard_map/all_gather | solution.py:69
  36.0 24.1 %all-gather.31.cloned.1.call-done = bf16[2048,512]{1,0:T(8,128)(2,1)} async-done(((bf16[512,512]{1,0:T(8,128)(2,1)}), bf16[2048,512]{1,0:T(8,128)(2,1)}) %all-gather.31.cloned.1.call-update) | async-done | bytes 2097168 | tf_op jit(solution)/shard_map/all_gather | solution.py:80
  67.9 16.4 all-gather.25.cloned.1.call-done
  93.0 21.3 all-gather.33.cloned.1.call-done
  116.5 33.1 %all-gather.29.cloned.1.call-done = bf16[2048,1024]{1,0:T(8,128)(2,1)} async-done(((bf16[512,1024]{1,0:T(8,128)(2,1)}), bf16[2048,1024]{1,0:T(8,128)(2,1)}) %all-gather.29.cloned.1.call-update) | async-done | bytes 4194320 | tf_op jit(solution)/shard_map/all_gather | solution.py:80
  155.7 25.8 %all-gather.27.cloned.1.call-done = bf16[1024,512]{0,1:T(8,128)(2,1)} async-done(((bf16[256,512]{0,1:T(8,128)(2,1)}), bf16[1024,512]{0,1:T(8,128)(2,1)}) %all-gather.27.cloned.1.call-update) | async-done | bytes 1048592 | tf_op jit(solution)/shard_map/all_gather | solution.py:193
  194.4 21.5 all-gather.35.cloned.1.call-done
  220.9 31.1 %all-gather.37.cloned.1.call-done = bf16[1024,2048]{1,0:T(8,128)(2,1)} async-done(((bf16[256,2048]{1,0:T(8,128)(2,1)}), bf16[1024,2048]{1,0:T(8,128)(2,1)}) %all-gather.37.cloned.1.call-update) | async-done | bytes 4194320 | tf_op jit(solution)/shard_map/all_gather | solution.py:80
  258.5 18.6 reduce-scatter.10.cloned.1.call-done
  283.8 18.6 all-gather.39.cloned.1.call-done
  302.4 83.7 %all-gather.41.cloned.1.call-done = bf16[2048,3072]{1,0:T(8,128)(2,1)} async-done(((bf16[512,3072]{1,0:T(8,128)(2,1)}), bf16[2048,3072]{1,0:T(8,128)(2,1)}) %all-gather.41.cloned.1.call-update) | async-done | bytes 12582928 | tf_op jit(solution)/shard_map/all_gather | solution.py:80
  396.0 73.5 %all-gather.43.cloned.1.call-done = bf16[2048,3072]{1,0:T(8,128)(2,1)} async-done(((bf16[512,3072]{1,0:T(8,128)(2,1)}), bf16[2048,3072]{1,0:T(8,128)(2,1)}) %all-gather.43.cloned.1.call-update) | async-done | bytes 12582928 | tf_op jit(solution)/shard_map/all_gather | solution.py:80
  479.6 13.4 all-gather.47.cloned.1.call-done
  493.0 83.5 %all-gather.45.cloned.1.call-done = bf16[3072,2048]{1,0:T(8,128)(2,1)} async-done(((bf16[768,2048]{1,0:T(8,128)(2,1)}), bf16[3072,2048]{1,0:T(8,128)(2,1)}) %all-gather.45.cloned.1.call-update) | async-done | bytes 12582928 | tf_op jit(solution)/shard_map/all_gather | solution.py:80
  576.6 13.4 multiply_convert_fusion
  606.3 20.5 reduce-scatter.14.cloned.1.call-done
  633.5 20.1 all-gather.49.cloned.1.call-done
  684.0 10.1 convolution_convert_fusion
  735.6 29.4 %pad_maximum_fusion.1 = bf16[2048,3072]{0,1:T(8,128)(2,1)} fusion(bf16[2048,1024]{0,1:T(8,128)(2,1)S(1)} %copy-done.3, bf16[2048,512]{0,1:T(8,128)(2,1)S(1)} %convolution_convert_fusion.6, bf16[2048,512]{0,1:T(8,128)(2,1)S(1)} %convolution_convert_fusion.7, bf16[2048,1024]{0,1:T(8,128)(2,1)S(1)} %copy-done.4), kind=kLoop, calls=%fused_computation.1 | loop fusion | flops 50331648 | bytes 25165824 | tf_op jit(solution)/shard_map/concatenate | solution.py:107
  782.3 20.4 pad_maximum_fusion
  823.0 49.0 %reduce-scatter.26.cloned.1.call-done = bf16[768,2048]{1,0:T(8,128)(2,1)} async-done(((bf16[3072,2048]{1,0:T(8,128)(2,1)}), bf16[768,2048]{1,0:T(8,128)(2,1)}) %reduce-scatter.26.cloned.1.call-update) | async-done | bytes 3145744 | tf_op jit(solution)/shard_map/reduce_scatter | solution.py:106
  872.0 99.6 %reduce-scatter.20.cloned.1.call-done = bf16[512,3072]{0,1:T(8,128)(2,1)} async-done(((bf16[2048,3072]{0,1:T(8,128)(2,1)}), bf16[512,3072]{0,1:T(8,128)(2,1)}) %reduce-scatter.20.cloned.1.call-update) | async-done | bytes 3145744 | tf_op jit(solution)/shard_map/reduce_scatter | solution.py:106
  971.6 184.5 %reduce-scatter.24.cloned.1.call-done = bf16[512,6144]{1,0:T(8,128)(2,1)} async-done(((bf16[2048,6144]{1,0:T(8,128)(2,1)}), bf16[512,6144]{1,0:T(8,128)(2,1)}) %reduce-scatter.24.cloned.1.call-update) | async-done | bytes 6291472 | tf_op jit(solution)/shard_map/reduce_scatter | solution.py:106
  1164.3 15.0 reduce-scatter.18.cloned.1.call-done
  1180.8 40.3 %all-reduce = (f32[2048]{0:T(1024)}, f32[128]{0:T(128)}, f32[128]{0:T(128)}, f32[2048]{0:T(1024)}) all-reduce(f32[2048]{0:T(1024)S(1)} %get-tuple-element.30, f32[128]{0:T(128)S(1)} %fusion.51, f32[128]{0:T(128)S(1)} %fusion.62, f32[2048]{0:T(1024)S(1)} %copy-done.46), channel_id=1, replica_groups=mesh['fsdp'=4,'ctx'=4,'tp'=2] {'fsdp','ctx','tp'}, use_global_device_ids=true, to_apply=%region_17.18 | all-reduce | flops 4352 | bytes 34816 | tf_op jit(solution)/shard_map/psum | solution.py:303
  1224.6 60.4 %all-gather.53.cloned.1.call-done = bf16[1024,2048]{1,0:T(8,128)(2,1)} async-done(((bf16[256,2048]{1,0:T(8,128)(2,1)}), bf16[1024,2048]{1,0:T(8,128)(2,1)}) %all-gather.53.cloned.1.call-update) | async-done | bytes 4194320 | tf_op jit(solution)/shard_map/all_gather | solution.py:13
  1289.6 213.6 %all-gather.57.cloned.1.call-done = bf16[3072,2048]{1,0:T(8,128)(2,1)} async-done(((bf16[768,2048]{1,0:T(8,128)(2,1)}), bf16[3072,2048]{1,0:T(8,128)(2,1)}) %all-gather.57.cloned.1.call-update) | async-done | bytes 12582928 | tf_op jit(solution)/shard_map/all_gather | solution.py:13
  1515.8 205.3 %all-gather.51.cloned.1.call-done = bf16[2048,3072]{0,1:T(8,128)(2,1)} async-done(((bf16[512,3072]{0,1:T(8,128)(2,1)}), bf16[2048,3072]{0,1:T(8,128)(2,1)}) %all-gather.51.cloned.1.call-update) | async-done | bytes 12582928 | tf_op jit(solution)/shard_map/all_gather | solution.py:13
  1721.1 22.0 %reshape.307 = bf16[4,512,3072]{1,0,2:T(4,128)(2,1)} reshape(bf16[2048,3072]{0,1:T(8,128)(2,1)} %all-gather.51.cloned.1.call-done) | data formatting | bytes 25165824 | tf_op jit(solution)/shard_map/all_gather | solution.py:13
  1743.1 19.9 reduce_sum.203
  1777.3 368.6 %all-gather.55.cloned.1.call-done = bf16[2048,6144]{1,0:T(8,128)(2,1)} async-done(((bf16[512,6144]{1,0:T(8,128)(2,1)}), bf16[2048,6144]{1,0:T(8,128)(2,1)}) %all-gather.55.cloned.1.call-update) | async-done | bytes 25165840 | tf_op jit(solution)/shard_map/all_gather | solution.py:13
  2145.9 17.7 reduce_sum.206
  (299 shorter events, 265.9 us)
Async XLA Ops:
  7.2 28.8 %all-gather.23.cloned.1.call-start = ((), (), s32[]{:S(2)}) async-start(), calls=%async_computation.9 | async-start | bytes 1572864 | tf_op jit(solution)/shard_map/all_gather | solution.py:69
  11.8 48.3 %all-gather.31.cloned.1.call-start = ((), (), s32[]{:S(2)}) async-start(), calls=%async_computation.13 | async-start | bytes 2621440 | tf_op jit(solution)/shard_map/all_gather | solution.py:80
  12.6 71.7 %all-gather.25.cloned.1.call-start = ((), (), s32[]{:S(2)}) async-start(), calls=%async_computation.10 | async-start | bytes 2621440 | tf_op jit(solution)/shard_map/all_gather | solution.py:80
  13.3 101.0 %all-gather.33.cloned.1.call-start = ((), (), s32[]{:S(2)}) async-start(), calls=%async_computation.14 | async-start | bytes 1310720 | tf_op jit(solution)/shard_map/all_gather | solution.py:194
  63.5 86.1 %all-gather.29.cloned.1.call-start = ((), (), s32[]{:S(2)}) async-start(), calls=%async_computation.12 | async-start | bytes 5242880 | tf_op jit(solution)/shard_map/all_gather | solution.py:80
  64.1 117.5 %all-gather.27.cloned.1.call-start = ((), (), s32[]{:S(2)}) async-start(), calls=%async_computation.11 | async-start | bytes 1310720 | tf_op jit(solution)/shard_map/all_gather | solution.py:193
  67.9 87.1 %copy-start.27 = (f32[256,64]{1,0:T(8,128)}, f32[256,64]{1,0:T(8,128)S(1)}, u32[]{:S(2)}) copy-start(f32[256,64]{1,0:T(8,128)S(1)} %get-tuple-element.67) | copy-start | bytes 196612
  89.3 126.6 %all-gather.35.cloned.1.call-start = ((), (), s32[]{:S(2)}) async-start(), calls=%async_computation.15 | async-start | bytes 5242880 | tf_op jit(solution)/shard_map/all_gather | solution.py:80
  90.1 161.9 %all-gather.37.cloned.1.call-start = ((), (), s32[]{:S(2)}) async-start(), calls=%async_computation.16 | async-start | bytes 5242880 | tf_op jit(solution)/shard_map/all_gather | solution.py:80
  90.8 186.3 %reduce-scatter.10.cloned.1.call-start = ((), (), s32[]{:S(2)}) async-start(), calls=%async_computation.17 | async-start | bytes 1572864 | tf_op jit(solution)/shard_map/reduce_scatter | solution.py:73
  91.4 63.2 %copy-start.57 = (f32[128]{0:T(128)}, f32[128]{0:T(128)S(1)}, u32[]{:S(2)}) copy-start(f32[128]{0:T(128)S(1)} %convert_element_type.161) | copy-start | bytes 1540
  256.6 45.8 %all-gather.39.cloned.1.call-start = ((), (), s32[]{:S(2)}) async-start(), calls=%async_computation.18 | async-start | bytes 1572864 | tf_op jit(solution)/shard_map/all_gather | solution.py:69
  280.9 105.1 %all-gather.41.cloned.1.call-start = ((), (), s32[]{:S(2)}) async-start(), calls=%async_computation.19 | async-start | bytes 15728640 | tf_op jit(solution)/shard_map/all_gather | solution.py:80
  281.7 187.9 %all-gather.43.cloned.1.call-start = ((), (), s32[]{:S(2)}) async-start(), calls=%async_computation.20 | async-start | bytes 15728640 | tf_op jit(solution)/shard_map/all_gather | solution.py:80
  282.3 210.7 %all-gather.47.cloned.1.call-start = ((), (), s32[]{:S(2)}) async-start(), calls=%async_computation.23 | async-start | bytes 1572864 | tf_op jit(solution)/shard_map/all_gather | solution.py:69
  283.0 293.5 %all-gather.45.cloned.1.call-start = ((), (), s32[]{:S(2)}) async-start(), calls=%async_computation.21 | async-start | bytes 15728640 | tf_op jit(solution)/shard_map/all_gather | solution.py:80
  283.6 343.2 %reduce-scatter.14.cloned.1.call-start = ((), (), s32[]{:S(2)}) async-start(), calls=%async_computation.24 | async-start | bytes 1572864 | tf_op jit(solution)/shard_map/reduce_scatter | solution.py:73
  606.3 47.3 %all-gather.49.cloned.1.call-start = ((), (), s32[]{:S(2)}) async-start(), calls=%async_computation.25 | async-start | bytes 1572864 | tf_op jit(solution)/shard_map/all_gather | solution.py:69
  632.2 90.8 %reduce-scatter.16.cloned.1.call-start = ((), (), s32[]{:S(2)}) async-start(), calls=%async_computation.26 | async-start | bytes 2621440 | tf_op jit(solution)/shard_map/reduce_scatter | solution.py:279
  679.2 143.3 %reduce-scatter.22.cloned.1.call-start = ((), (), s32[]{:S(2)}) async-start(), calls=%async_computation.29 | async-start | bytes 5242880 | tf_op jit(solution)/shard_map/reduce_scatter | solution.py:106
  683.9 188.0 %reduce-scatter.26.cloned.1.call-start = ((), (), s32[]{:S(2)}) async-start(), calls=%async_computation.31 | async-start | bytes 15728640 | tf_op jit(solution)/shard_map/reduce_scatter | solution.py:106
  694.1 277.5 %reduce-scatter.20.cloned.1.call-start = ((), (), s32[]{:S(2)}) async-start(), calls=%async_computation.28 | async-start | bytes 15728640 | tf_op jit(solution)/shard_map/reduce_scatter | solution.py:106
  765.0 391.1 %reduce-scatter.24.cloned.1.call-start = ((), (), s32[]{:S(2)}) async-start(), calls=%async_computation.30 | async-start | bytes 31457280 | tf_op jit(solution)/shard_map/reduce_scatter | solution.py:106
  802.7 376.6 %reduce-scatter.18.cloned.1.call-start = ((), (), s32[]{:S(2)}) async-start(), calls=%async_computation.27 | async-start | bytes 1572864 | tf_op jit(solution)/shard_map/reduce_scatter | solution.py:73
  812.6 408.6 %reduce-scatter.12.cloned.1.call-start = ((), (), s32[]{:S(2)}) async-start(), calls=%async_computation.22 | async-start | bytes 1572864 | tf_op jit(solution)/shard_map/reduce_scatter | solution.py:73
  822.4 462.6 %all-gather.53.cloned.1.call-start = ((), (), s32[]{:S(2)}) async-start(), calls=%async_computation.33 | async-start | bytes 5242880 | tf_op jit(solution)/shard_map/all_gather | solution.py:13
  822.9 680.3 %all-gather.57.cloned.1.call-start = ((), (), s32[]{:S(2)}) async-start(), calls=%async_computation.35 | async-start | bytes 15728640 | tf_op jit(solution)/shard_map/all_gather | solution.py:13
  872.0 849.1 %all-gather.51.cloned.1.call-start = ((), (), s32[]{:S(2)}) async-start(), calls=%async_computation.32 | async-start | bytes 15728640 | tf_op jit(solution)/shard_map/all_gather | solution.py:13
  971.6 1174.3 %all-gather.55.cloned.1.call-start = ((), (), s32[]{:S(2)}) async-start(), calls=%async_computation.34 | async-start | bytes 31457280 | tf_op jit(solution)/shard_map/all_gather | solution.py:13
  1158.2 63.0 %copy-start.48 = (f32[128]{0:T(128)S(1)}, f32[128]{0:T(128)}, u32[]{:S(2)}) copy-start(f32[128]{0:T(128)} %compare_convert_fusion) | copy-start | bytes 1540
  1158.2 63.0 %copy-start.51 = (f32[128]{0:T(128)S(1)}, f32[128]{0:T(128)}, u32[]{:S(2)}) copy-start(f32[128]{0:T(128)} %copy-done.50) | copy-start | bytes 1540
  1158.2 63.0 %copy-start.61 = (f32[128]{0:T(128)S(1)}, f32[128]{0:T(128)}, u32[]{:S(2)}) copy-start(f32[128]{0:T(128)} %copy-done.60) | copy-start | bytes 1540
  (60 other events, 673.4 us)
Sparse Core Ops, SparseCore 0:
  11.9 23.9 all-gather.22
  37.5 22.5 all-gather.30
  61.7 22.5 all-gather.24
  86.3 27.9 all-gather.32
  115.7 33.8 all-gather.28
  151.6 29.9 all-gather.26
  183.1 32.7 all-gather.34
  217.5 34.4 all-gather.36
  256.7 20.3 reduce-scatter.9
  281.1 21.2 all-gather.38
  303.9 82.0 all-gather.40
  387.4 82.0 all-gather.42
  471.7 21.2 all-gather.46
  494.4 82.0 all-gather.44
  606.4 20.3 reduce-scatter.13
  632.3 21.2 all-gather.48
  679.3 43.5 reduce-scatter.15
  725.9 43.7 reduce-scatter.21
  772.3 99.6 reduce-scatter.25
  874.4 97.1 reduce-scatter.19
  974.2 181.8 reduce-scatter.23
  1158.9 20.3 reduce-scatter.17
  1182.2 20.5 reduce-scatter.11
  1204.3 80.6 all-gather.52
  1286.5 216.6 all-gather.56
  1504.7 216.3 all-gather.50
  1722.5 423.3 all-gather.54
